TPU v7x, 128 devices: a whole 4x4x4 slice. The times are simulated.
128 devices in a mesh: prow: 8 (over y, core), pcol: 16 (over x, z).
Axes of the slice: x: 4, y: 4, z: 4, core: 2. Of those that a mesh axis runs over, the one named last changes fastest.
Arguments:
- cross_cov: float32 [2, 512, 16384], P(None, 'prow', 'pcol'), may hold values from -6 to 6
- prev_rows: bfloat16 [2, 512, 32768], P(None, 'pcol', 'prow'), may hold values from -0.046875 to 0.046875
- prev_solved: bfloat16 [32768, 16384], P('prow', 'pcol'), may hold values from -6 to 6
- sub_block: float32 [512, 512], replicated, may hold values from -0.25 to 0.25
- inv_first: float32 [512, 512], replicated, as said below
- inv_second: float32 [512, 512], replicated, as said below
Outputs:
- solved: float32 [2, 512, 16384], P(None, 'prow', 'pcol')
Inputs may be any that keep to these rules, and one draw needn't show every extreme that they name: inv_first is lower triangular with a positive diagonal. inv_second is lower triangular with a positive diagonal.
All inputs are finite; a program needn't handle non-finite values.
Results may differ from a plain program's by a relative error of at most 0.0003.
Values may be sent and summed in bfloat16 or wider, within the bound.
A program may use at most 64 MiB of HBM per device.

v0:
```python
import jax
import jax.numpy as jnp
from jax import lax
from jax.sharding import PartitionSpec as P


def mult(left, right):
    return jnp.dot(left, right, preferred_element_type=jnp.float32, precision=lax.Precision.HIGHEST)


def local(cross_cov, prev_rows, prev_solved, sub_block, inv_first, inv_second):
    terms = jnp.einsum(
        "kra,ac->krc",
        lax.all_gather(prev_rows, "pcol", axis=1, tiled=True),
        prev_solved,
        preferred_element_type=jnp.float32,
    )
    update = lax.psum_scatter(terms, "prow", scatter_dimension=1, tiled=True)
    first_part = cross_cov[0] - update[0]
    second_part = cross_cov[1] - update[1]
    local_rows = first_part.shape[0]
    offset = lax.axis_index("prow") * local_rows

    def own_rows(matrix):
        return lax.dynamic_slice_in_dim(matrix, offset, local_rows, 0)

    first_full = lax.all_gather(first_part, "prow", axis=0, tiled=True)
    solved_first = mult(own_rows(inv_first), first_full)
    solved_full = lax.all_gather(solved_first, "prow", axis=0, tiled=True)
    reduced = second_part - mult(own_rows(sub_block), solved_full)
    reduced_full = lax.all_gather(reduced, "prow", axis=0, tiled=True)
    solved_second = mult(own_rows(inv_second), reduced_full)
    return jnp.stack([solved_first, solved_second])


def solution(mesh):
    return jax.shard_map(
        local,
        mesh=mesh,
        in_specs=(
            P(None, "prow", "pcol"),
            P(None, "pcol", "prow"),
            P("prow", "pcol"),
            P(),
            P(),
            P(),
        ),
        out_specs=P(None, "prow", "pcol"),
        check_vma=False,
    )
```

profile of v0, /device:TPU:1, one launch (start us, length us, event | category | flops | bytes accessed | tf_op | source)
XLA Modules:
  0.0 231.8 jit_solution(13975077794349353256)
XLA Ops:
  6.5 0.0 copy-start
  6.5 0.0 all-gather.6.cloned.1.call-start
  6.5 0.7 all-gather.6.cloned.1.call-update
  7.3 0.0 reduce-scatter.2.cloned.1.call-start
  7.3 76.4 %all-gather.6.cloned.1.call-done = bf16[2,512,4096]{2,1,0:T(8,128)(2,1)} async-done(((bf16[2,32,4096]{2,1,0:T(8,128)(2,1)}), bf16[2,512,4096]{2,1,0:T(8,128)(2,1)}) %all-gather.6.cloned.1.call-update) | async-done | bytes 8388624 | tf_op jit(solution)/shard_map/all_gather | solution.py:14
  83.7 15.0 %fusion = f32[2,512,1024]{2,1,0:T(8,128)} fusion(bf16[2,512,4096]{2,1,0:T(8,128)(2,1)} %all-gather.6.cloned.1.call-done, bf16[4096,1024]{1,0:T(8,128)(2,1)} %param.8), kind=kOutput, calls=%fused_computation | convolution fusion | flops 8589934592 | bytes 20971520 | tf_op jit(solution)/shard_map/kra,ac->krc/dot_general | solution.py:12
  98.7 0.0 reduce-scatter.2.cloned.1.call-update
  98.7 0.0 all-gather.12.cloned.1.call-start
  98.8 34.5 %reduce-scatter.2.cloned.1.call-done = f32[2,64,1024]{2,1,0:T(8,128)} async-done(((f32[2,512,1024]{2,1,0:T(8,128)}), f32[2,64,1024]{2,1,0:T(8,128)}) %reduce-scatter.2.cloned.1.call-update) | async-done | bytes 524304 | tf_op jit(solution)/shard_map/reduce_scatter | solution.py:18
  133.3 0.0 copy-done.2
  133.3 1.8 slice_subtract_fusion.1
  135.1 0.0 all-gather.12.cloned.1.call-update
  135.1 0.0 all-gather.8.cloned.1.call-start
  135.2 27.5 %all-gather.12.cloned.1.call-done = f32[1,512,1024]{2,1,0:T(8,128)} async-done(((f32[1,64,1024]{2,1,0:T(8,128)}), f32[1,512,1024]{2,1,0:T(8,128)}) %all-gather.12.cloned.1.call-update) | async-done | bytes 2097168 | tf_op jit(solution)/shard_map/all_gather | solution.py:27
  162.7 0.0 copy-done
  162.7 3.7 %fusion.2 = f32[64,1024]{1,0:T(8,128)} fusion(f32[1,512,1024]{2,1,0:T(8,128)} %all-gather.12.cloned.1.call-done, f32[512,512]{1,0:T(8,128)S(1)} %copy-done, s32[]{:T(128)S(6)} %select_n.2), kind=kOutput, calls=%fused_computation.2 | convolution fusion | flops 402653184 | bytes 2490372 | tf_op jit(solution)/shard_map/dot_general | solution.py:8
  166.4 0.0 all-gather.8.cloned.1.call-update
  166.4 0.0 all-gather.10.cloned.1.call-start
  166.4 25.6 %all-gather.8.cloned.1.call-done = f32[512,1024]{1,0:T(8,128)} async-done(((f32[64,1024]{1,0:T(8,128)}), f32[512,1024]{1,0:T(8,128)}) %all-gather.8.cloned.1.call-update) | async-done | bytes 2097168 | tf_op jit(solution)/shard_map/all_gather | solution.py:29
  192.0 3.8 %convolution_subtract_fusion = f32[64,1024]{1,0:T(8,128)} fusion(f32[512,1024]{1,0:T(8,128)} %all-gather.8.cloned.1.call-done, f32[2,64,1024]{2,1,0:T(8,128)S(1)} %copy-done.3, f32[2,64,1024]{2,1,0:T(8,128)S(1)} %copy-done.2, f32[512,512]{1,0:T(8,128)} %param.9, s32[]{:T(128)S(6)} %select_n.2), kind=kOutput, calls=%fused_computation.4 | convolution fusion | flops 402784256 | bytes 3014660 | tf_op jit(solution)/shard_map/dot_general | solution.py:8
  195.8 0.0 all-gather.10.cloned.1.call-update
  195.8 25.6 %all-gather.10.cloned.1.call-done = f32[512,1024]{1,0:T(8,128)} async-done(((f32[64,1024]{1,0:T(8,128)}), f32[512,1024]{1,0:T(8,128)}) %all-gather.10.cloned.1.call-update) | async-done | bytes 2097168 | tf_op jit(solution)/shard_map/all_gather | solution.py:31
  221.4 3.0 %convolution_bitcast_fusion = f32[1,64,1024]{2,1,0:T(8,128)S(1)} fusion(f32[512,1024]{1,0:T(8,128)} %all-gather.10.cloned.1.call-done, f32[512,512]{1,0:T(8,128)} %param.11, s32[]{:T(128)S(6)} %select_n.2), kind=kOutput, calls=%fused_computation.5 | convolution fusion | flops 402653184 | bytes 2490372 | tf_op jit(solution)/shard_map/dot_general | solution.py:8
  224.5 0.8 pad_maximum_fusion
  (5 shorter events, 0.0 us)
Async XLA Ops:
  6.5 156.2 %copy-start = (f32[512,512]{1,0:T(8,128)S(1)}, f32[512,512]{1,0:T(8,128)}, u32[]{:S(2)}) copy-start(f32[512,512]{1,0:T(8,128)} %param.10) | copy-start | bytes 3145732
  6.5 77.1 %all-gather.6.cloned.1.call-start = ((), (), s32[]{:S(2)}) async-start(), calls=%async_computation.1 | async-start | bytes 8912896 | tf_op jit(solution)/shard_map/all_gather | solution.py:14
  7.3 126.1 %reduce-scatter.2.cloned.1.call-start = ((), (), s32[]{:S(2)}) async-start(), calls=%async_computation.2 | async-start | bytes 4718592 | tf_op jit(solution)/shard_map/reduce_scatter | solution.py:18
  98.7 34.6 %copy-start.2 = (f32[2,64,1024]{2,1,0:T(8,128)S(1)}, f32[2,64,1024]{2,1,0:T(8,128)}, u32[]{:S(2)}) copy-start(f32[2,64,1024]{2,1,0:T(8,128)} %param.6) | copy-start | bytes 1572868
  98.7 64.0 %all-gather.12.cloned.1.call-start = ((), (), s32[]{:S(2)}) async-start(), calls=%async_computation.5 | async-start | bytes 2359296 | tf_op jit(solution)/shard_map/all_gather | solution.py:27
  133.3 58.7 %copy-start.3 = (f32[2,64,1024]{2,1,0:T(8,128)S(1)}, f32[2,64,1024]{2,1,0:T(8,128)}, u32[]{:S(2)}) copy-start(f32[2,64,1024]{2,1,0:T(8,128)} %reduce-scatter.2.cloned.1.call-done) | copy-start | bytes 1572868
  135.1 56.9 %all-gather.8.cloned.1.call-start = ((), (), s32[]{:S(2)}) async-start(), calls=%async_computation.3 | async-start | bytes 2359296 | tf_op jit(solution)/shard_map/all_gather | solution.py:29
  166.4 55.0 %all-gather.10.cloned.1.call-start = ((), (), s32[]{:S(2)}) async-start(), calls=%async_computation.4 | async-start | bytes 2359296 | tf_op jit(solution)/shard_map/all_gather | solution.py:31
  195.8 28.7 %copy-start.1 = (f32[64,1024]{1,0:T(8,128)S(1)}, f32[64,1024]{1,0:T(8,128)}, u32[]{:S(2)}) copy-start(f32[64,1024]{1,0:T(8,128)} %fusion.2) | copy-start | bytes 786436
Sparse Core Ops, SparseCore 0:
  9.6 74.0 all-gather.5
  98.8 34.4 reduce-scatter.1
  135.2 27.4 all-gather.11
  166.5 25.4 all-gather.7
  195.9 25.4 all-gather.9
where the time goes:
time: 232 us
  waiting for transfers between devices  190 us (82%)
  matrix products  25.5 us (11%)
  between operations  13.2 us (6%)
  other arithmetic  2.59 us (1%)
    all_gather x1, waiting for transfers between devices, local(): lax.all_gather(prev_rows, 'pcol', axis=1, tiled=True)  76.4 us
    reduce_scatter x1, waiting for transfers between devices, local(): update = lax.psum_scatter(terms, 'prow', scatter_dimension=1, tiled=True)  34.5 us
    all_gather x1, waiting for transfers between devices, local(): first_full = lax.all_gather(first_part, 'prow', axis=0, tiled=True)  27.5 us
    all_gather x1, waiting for transfers between devices, local(): reduced_full = lax.all_gather(reduced, 'prow', axis=0, tiled=True)  25.6 us
    all_gather x1, waiting for transfers between devices, local(): solved_full = lax.all_gather(solved_first, 'prow', axis=0, tiled=True)  25.6 us
    dot_general x1, matrix products, local(): jnp.einsum('kra,ac->krc', lax.all_gather(prev_rows, 'pcol', axis=1, tiled...  15 us
    dot_general x3, matrix products, mult(): jnp.dot(left, right, preferred_element_type=jnp.float32, precision=lax.Pr...  10.5 us
  transfers between devices with their start and end apart: 5, of which 5 were waited for; matrix products, arithmetic and copies ran while one was open for 0% of the time, Pallas kernels for 0%

commit v1 on v0

--- a/solution.py
+++ b/solution.py
@@ -28,7 +28,16 @@
     solved_first = mult(own_rows(inv_first), first_full)
     solved_full = lax.all_gather(solved_first, "prow", axis=0, tiled=True)
     reduced = second_part - mult(own_rows(sub_block), solved_full)
-    reduced_full = lax.all_gather(reduced, "prow", axis=0, tiled=True)
+    ways = lax.axis_size("prow")
+    up = [(d, (d + 1) % ways) for d in range(ways)]
+    down = [(d, (d - 1) % ways) for d in range(ways)]
+    earlier, later = ([reduced], [reduced])
+    for _ in range(ways // 2):
+        earlier.append(lax.ppermute(earlier[-1], "prow", up))
+    for _ in range((ways - 1) // 2):
+        later.append(lax.ppermute(later[-1], "prow", down))
+    line = jnp.concatenate([*earlier[::-1], *later[1:]], axis=0)
+    reduced_full = jnp.roll(line, (lax.axis_index("prow") - ways // 2) * reduced.shape[0], axis=0)
     solved_second = mult(own_rows(inv_second), reduced_full)
     return jnp.stack([solved_first, solved_second])
 

time: 232 us -> 232 us (level); the launches traced: 232 us -> 229 us
  waiting for transfers between devices: 190 us -> 175 us
  starting transfers between devices: 0.17 us -> 13.9 us
    all_gather x1 -> x0, waiting for transfers between devices: 25.6 us -> none  [local(): reduced_full = lax.all_gather(reduced, 'prow', axis=0, tiled=True)]
    ppermute x0 -> x7, starting transfers between devices: none -> 13.8 us  [the longest x4 7.86 us: local(): earlier.append(lax.ppermute(earlier[-1], 'prow', up))]
    ppermute x0 -> x7, waiting for transfers between devices: none -> 10.2 us  [the longest x4 7.63 us: local(): earlier.append(lax.ppermute(earlier[-1], 'prow', up))]
  transfers between devices with their start and end apart: 5 -> 11, of which waited for: 5 -> 11; matrix products, arithmetic and copies ran while one was open for 0% -> 0% of each run, Pallas kernels for 0% -> 0%
where the time goes in v1:
time: 232 us; the launch traced here: 229 us
  waiting for transfers between devices  175 us (75%)
  matrix products  24 us (10%)
  starting transfers between devices  13.9 us (6%)
  between operations  13.3 us (6%)
  other arithmetic  2.52 us (1%)
    all_gather x1, waiting for transfers between devices, local(): lax.all_gather(prev_rows, 'pcol', axis=1, tiled=True)  76.4 us
    reduce_scatter x1, waiting for transfers between devices, local(): update = lax.psum_scatter(terms, 'prow', scatter_dimension=1, tiled=True)  34.5 us
    all_gather x1, waiting for transfers between devices, local(): first_full = lax.all_gather(first_part, 'prow', axis=0, tiled=True)  27.5 us
    all_gather x1, waiting for transfers between devices, local(): solved_full = lax.all_gather(solved_first, 'prow', axis=0, tiled=True)  25.6 us
    dot_general x1, matrix products, local(): jnp.einsum('kra,ac->krc', lax.all_gather(prev_rows, 'pcol', axis=1, tiled...  15 us
    dot_general x3, matrix products, mult(): jnp.dot(left, right, preferred_element_type=jnp.float32, precision=lax.Pr...  8.96 us
    ppermute x4, starting transfers between devices, local(): earlier.append(lax.ppermute(earlier[-1], 'prow', up))  7.86 us
    ppermute x4, waiting for transfers between devices, local(): earlier.append(lax.ppermute(earlier[-1], 'prow', up))  7.63 us
  transfers between devices with their start and end apart: 11, of which 11 were waited for; matrix products, arithmetic and copies ran while one was open for 0% of the time, Pallas kernels for 0%

profile of v1, /device:TPU:1, one launch (start us, length us, event | category | flops | bytes accessed | tf_op | source)
XLA Modules:
  0.0 229.0 jit_solution(16162558449653900317)
XLA Ops:
  6.5 0.7 all-gather.5.cloned.1.call-update
  7.3 76.4 %all-gather.5.cloned.1.call-done = bf16[2,512,4096]{2,1,0:T(8,128)(2,1)} async-done(((bf16[2,32,4096]{2,1,0:T(8,128)(2,1)}), bf16[2,512,4096]{2,1,0:T(8,128)(2,1)}) %all-gather.5.cloned.1.call-update) | async-done | bytes 8388624 | tf_op jit(solution)/shard_map/all_gather | solution.py:14
  83.7 15.0 %fusion = f32[2,512,1024]{2,1,0:T(8,128)} fusion(bf16[2,512,4096]{2,1,0:T(8,128)(2,1)} %all-gather.5.cloned.1.call-done, bf16[4096,1024]{1,0:T(8,128)(2,1)} %param.8), kind=kOutput, calls=%fused_computation | convolution fusion | flops 8589934592 | bytes 20971520 | tf_op jit(solution)/shard_map/kra,ac->krc/dot_general | solution.py:12
  98.8 34.5 %reduce-scatter.2.cloned.1.call-done = f32[2,64,1024]{2,1,0:T(8,128)} async-done(((f32[2,512,1024]{2,1,0:T(8,128)}), f32[2,64,1024]{2,1,0:T(8,128)}) %reduce-scatter.2.cloned.1.call-update) | async-done | bytes 524304 | tf_op jit(solution)/shard_map/reduce_scatter | solution.py:18
  133.3 1.7 slice_subtract_fusion.1
  135.1 27.5 %all-gather.9.cloned.1.call-done = f32[1,512,1024]{2,1,0:T(8,128)} async-done(((f32[1,64,1024]{2,1,0:T(8,128)}), f32[1,512,1024]{2,1,0:T(8,128)}) %all-gather.9.cloned.1.call-update) | async-done | bytes 2097168 | tf_op jit(solution)/shard_map/all_gather | solution.py:27
  162.6 3.7 %fusion.2 = f32[64,1024]{1,0:T(8,128)} fusion(f32[1,512,1024]{2,1,0:T(8,128)} %all-gather.9.cloned.1.call-done, f32[512,512]{1,0:T(8,128)S(1)} %copy-done, s32[]{:T(128)S(6)} %select_n.18), kind=kOutput, calls=%fused_computation.2 | convolution fusion | flops 402653184 | bytes 2490372 | tf_op jit(solution)/shard_map/dot_general | solution.py:8
  166.3 25.6 %all-gather.7.cloned.1.call-done = f32[512,1024]{1,0:T(8,128)} async-done(((f32[64,1024]{1,0:T(8,128)}), f32[512,1024]{1,0:T(8,128)}) %all-gather.7.cloned.1.call-update) | async-done | bytes 2097168 | tf_op jit(solution)/shard_map/all_gather | solution.py:29
  191.9 3.0 %convolution_subtract_fusion = f32[64,1024]{1,0:T(8,128)S(1)} fusion(f32[512,1024]{1,0:T(8,128)} %all-gather.7.cloned.1.call-done, f32[2,64,1024]{2,1,0:T(8,128)} %reduce-scatter.2.cloned.1.call-done, f32[2,64,1024]{2,1,0:T(8,128)S(1)} %copy-done.2, f32[512,512]{1,0:T(8,128)} %param.9, s32[]{:T(128)S(6)} %select_n.18), kind=kOutput, calls=%fused_computation.6 | convolution fusion | flops 402784256 | bytes 3014660 | tf_op jit(solution)/shard_map/dot_general | solution.py:8
  194.9 0.4 collective-permute-start
  195.3 3.3 %collective-permute-done = f32[64,1024]{1,0:T(8,128)S(1)} collective-permute-done((f32[64,1024]{1,0:T(8,128)S(1)}, f32[64,1024]{1,0:T(8,128)S(1)}, u32[]{:S(2)}, u32[]{:S(2)}) %collective-permute-start) | collective-permute-done | bytes 262176 | tf_op jit(solution)/shard_map/ppermute | solution.py:36
  198.6 2.5 %collective-permute-start.1 = (f32[64,1024]{1,0:T(8,128)S(1)}, f32[64,1024]{1,0:T(8,128)S(1)}, u32[]{:S(2)}, u32[]{:S(2)}) collective-permute-start(f32[64,1024]{1,0:T(8,128)S(1)} %collective-permute-done), channel_id=1, source_target_pairs={{0,16},{16,32},{32,48},{48,64},{64,80},{80,96},{96,112},{112,0},{1... | collective-permute-start | bytes 786440 | tf_op jit(solution)/shard_map/ppermute | solution.py:36
  201.1 1.1 collective-permute-start.4
  202.2 2.3 collective-permute-done.1
  204.4 2.5 %collective-permute-start.2 = (f32[64,1024]{1,0:T(8,128)S(1)}, f32[64,1024]{1,0:T(8,128)S(1)}, u32[]{:S(2)}, u32[]{:S(2)}) collective-permute-start(f32[64,1024]{1,0:T(8,128)S(1)} %collective-permute-done.1), channel_id=1, source_target_pairs={{0,16},{16,32},{32,48},{48,64},{64,80},{80,96},{96,112},{112,0},{1... | collective-permute-start | bytes 786440 | tf_op jit(solution)/shard_map/ppermute | solution.py:36
  207.2 2.0 collective-permute-start.5
  209.2 1.0 collective-permute-done.2
  210.2 2.5 %collective-permute-start.3 = (f32[64,1024]{1,0:T(8,128)S(1)}, f32[64,1024]{1,0:T(8,128)S(1)}, u32[]{:S(2)}, u32[]{:S(2)}) collective-permute-start(f32[64,1024]{1,0:T(8,128)S(1)} %collective-permute-done.2), channel_id=1, source_target_pairs={{0,16},{16,32},{32,48},{48,64},{64,80},{80,96},{96,112},{112,0},{1... | collective-permute-start | bytes 786440 | tf_op jit(solution)/shard_map/ppermute | solution.py:36
  212.7 0.6 collective-permute-done.5
  213.3 2.9 %collective-permute-start.6 = (f32[64,1024]{1,0:T(8,128)S(1)}, f32[64,1024]{1,0:T(8,128)S(1)}, u32[]{:S(2)}, u32[]{:S(2)}) collective-permute-start(f32[64,1024]{1,0:T(8,128)S(1)} %collective-permute-done.5), channel_id=1, source_target_pairs={{0,112},{16,0},{32,16},{48,32},{64,48},{80,64},{96,80},{112,96},{1... | collective-permute-start | bytes 786440 | tf_op jit(solution)/shard_map/ppermute | solution.py:38
  216.2 1.0 collective-permute-done.3
  217.4 1.7 collective-permute-done.6
  219.4 2.3 %fusion.6 = f32[1,64,1024]{2,1,0:T(8,128)S(1)} fusion(f32[1024,1024]{1,0:T(8,128)S(1)} %constant_dynamic-update-slice_fusion, s32[]{:T(128)S(6)} %select_n.20, f32[512,512]{1,0:T(8,128)} %param.11, s32[]{:T(128)S(6)} %select_n.18), kind=kOutput, calls=%fused_computation.7 | convolution fusion | flops 402653184 | bytes 2490376 | tf_op jit(solution)/shard_map/dot_general | solution.py:8
  221.7 0.8 pad_maximum_fusion
  (30 shorter events, 0.8 us)
Async XLA Ops:
  6.5 156.1 %copy-start = (f32[512,512]{1,0:T(8,128)S(1)}, f32[512,512]{1,0:T(8,128)}, u32[]{:S(2)}) copy-start(f32[512,512]{1,0:T(8,128)} %param.10) | copy-start | bytes 3145732
  6.5 77.1 %all-gather.5.cloned.1.call-start = ((), (), s32[]{:S(2)}) async-start(), calls=%async_computation.1 | async-start | bytes 8912896 | tf_op jit(solution)/shard_map/all_gather | solution.py:14
  7.3 126.1 %reduce-scatter.2.cloned.1.call-start = ((), (), s32[]{:S(2)}) async-start(), calls=%async_computation.2 | async-start | bytes 4718592 | tf_op jit(solution)/shard_map/reduce_scatter | solution.py:18
  98.7 34.6 %copy-start.2 = (f32[2,64,1024]{2,1,0:T(8,128)S(1)}, f32[2,64,1024]{2,1,0:T(8,128)}, u32[]{:S(2)}) copy-start(f32[2,64,1024]{2,1,0:T(8,128)} %param.6) | copy-start | bytes 1572868
  98.7 63.9 %all-gather.9.cloned.1.call-start = ((), (), s32[]{:S(2)}) async-start(), calls=%async_computation.4 | async-start | bytes 2359296 | tf_op jit(solution)/shard_map/all_gather | solution.py:27
  135.0 56.9 %all-gather.7.cloned.1.call-start = ((), (), s32[]{:S(2)}) async-start(), calls=%async_computation.3 | async-start | bytes 2359296 | tf_op jit(solution)/shard_map/all_gather | solution.py:29
  194.9 3.7 %collective-permute-start = (f32[64,1024]{1,0:T(8,128)S(1)}, f32[64,1024]{1,0:T(8,128)S(1)}, u32[]{:S(2)}, u32[]{:S(2)}) collective-permute-start(f32[64,1024]{1,0:T(8,128)S(1)} %convolution_subtract_fusion), channel_id=1, source_target_pairs={{0,16},{16,32},{32,48},{48,64},{64,80},{80,96},{96,112},{112,0},{1... | collective-permute-start | bytes 786440 | tf_op jit(solution)/shard_map/ppermute | solution.py:36
  198.6 5.8 %collective-permute-start.1 = (f32[64,1024]{1,0:T(8,128)S(1)}, f32[64,1024]{1,0:T(8,128)S(1)}, u32[]{:S(2)}, u32[]{:S(2)}) collective-permute-start(f32[64,1024]{1,0:T(8,128)S(1)} %collective-permute-done), channel_id=1, source_target_pairs={{0,16},{16,32},{32,48},{48,64},{64,80},{80,96},{96,112},{112,0},{1... | collective-permute-start | bytes 786440 | tf_op jit(solution)/shard_map/ppermute | solution.py:36
  201.1 6.1 %collective-permute-start.4 = (f32[64,1024]{1,0:T(8,128)S(1)}, f32[64,1024]{1,0:T(8,128)S(1)}, u32[]{:S(2)}, u32[]{:S(2)}) collective-permute-start(f32[64,1024]{1,0:T(8,128)S(1)} %convolution_subtract_fusion), channel_id=1, source_target_pairs={{0,112},{16,0},{32,16},{48,32},{64,48},{80,64},{96,80},{112,96},{1... | collective-permute-start | bytes 786440 | tf_op jit(solution)/shard_map/ppermute | solution.py:38
  204.4 5.8 %collective-permute-start.2 = (f32[64,1024]{1,0:T(8,128)S(1)}, f32[64,1024]{1,0:T(8,128)S(1)}, u32[]{:S(2)}, u32[]{:S(2)}) collective-permute-start(f32[64,1024]{1,0:T(8,128)S(1)} %collective-permute-done.1), channel_id=1, source_target_pairs={{0,16},{16,32},{32,48},{48,64},{64,80},{80,96},{96,112},{112,0},{1... | collective-permute-start | bytes 786440 | tf_op jit(solution)/shard_map/ppermute | solution.py:36
  207.2 6.1 %collective-permute-start.5 = (f32[64,1024]{1,0:T(8,128)S(1)}, f32[64,1024]{1,0:T(8,128)S(1)}, u32[]{:S(2)}, u32[]{:S(2)}) collective-permute-start(f32[64,1024]{1,0:T(8,128)S(1)} %collective-permute-done.4), channel_id=1, source_target_pairs={{0,112},{16,0},{32,16},{48,32},{64,48},{80,64},{96,80},{112,96},{1... | collective-permute-start | bytes 786440 | tf_op jit(solution)/shard_map/ppermute | solution.py:38
  210.2 7.0 %collective-permute-start.3 = (f32[64,1024]{1,0:T(8,128)S(1)}, f32[64,1024]{1,0:T(8,128)S(1)}, u32[]{:S(2)}, u32[]{:S(2)}) collective-permute-start(f32[64,1024]{1,0:T(8,128)S(1)} %collective-permute-done.2), channel_id=1, source_target_pairs={{0,16},{16,32},{32,48},{48,64},{64,80},{80,96},{96,112},{112,0},{1... | collective-permute-start | bytes 786440 | tf_op jit(solution)/shard_map/ppermute | solution.py:36
  213.3 5.8 %collective-permute-start.6 = (f32[64,1024]{1,0:T(8,128)S(1)}, f32[64,1024]{1,0:T(8,128)S(1)}, u32[]{:S(2)}, u32[]{:S(2)}) collective-permute-start(f32[64,1024]{1,0:T(8,128)S(1)} %collective-permute-done.5), channel_id=1, source_target_pairs={{0,112},{16,0},{32,16},{48,32},{64,48},{80,64},{96,80},{112,96},{1... | collective-permute-start | bytes 786440 | tf_op jit(solution)/shard_map/ppermute | solution.py:38
  217.4 4.3 %copy-start.1 = (f32[64,1024]{1,0:T(8,128)S(1)}, f32[64,1024]{1,0:T(8,128)}, u32[]{:S(2)}) copy-start(f32[64,1024]{1,0:T(8,128)} %fusion.2) | copy-start | bytes 786436
Sparse Core Ops, SparseCore 0:
  9.6 74.0 all-gather.4
  98.8 34.4 reduce-scatter.1
  135.1 27.4 all-gather.8
  166.4 25.4 all-gather.6
